TPU v7x, 32 devices: a whole 2x2x4 slice. The times are simulated.
32 devices in a mesh: dom: 2 (over y), row: 4 (over z), sub: 2 (over x), rep: 2 (over core).
Axes of the slice: x: 2, y: 2, z: 4, core: 2. Of those that a mesh axis runs over, the one named last changes fastest.
Arguments:
- vectors: bfloat16 [28672, 768], P(('dom', 'row', 'sub', 'rep')), parts along dimension 0, may hold values from -150 to 150
- rotation: bfloat16 [1536, 768], P('dom'), parts along dimension 0, may hold values from -0.21875 to 0.21875
- codebooks: float32 [96, 256, 16], P(('dom', 'sub')), parts along dimension 0, may hold values from -8 to 8
Outputs:
- reconstruction: bfloat16 [28672, 768], P(('dom', 'row', 'sub', 'rep')), parts along dimension 0
- new_codebooks: float32 [96, 256, 16], P(('dom', 'sub')), parts along dimension 0
- cross_cov: float32 [1536, 768], P(('dom', 'sub')), parts along dimension 0
There are 2 independent parts, one for each index of `dom`. A program takes and returns all parts, laid end to end along the dimension named above; each array names one. Nothing has to cross between parts.
All inputs are finite; a program needn't handle non-finite values.
Results may differ from a plain program's by a relative error of at most 0.012.
Values may be sent and summed in bfloat16 or wider, within the bound.
No kernel may reach another device: no remote copies, remote signals or barrier semaphores. Data moves between devices by JAX's collectives and lax.ppermute only.
A program may use at most 64 MiB of HBM per device.

v0:
```python
import jax
import jax.numpy as jnp
from jax import lax
from jax.sharding import PartitionSpec as P

SUBDIM = 16
softness_scale = 4.0


def quantize_rows(block, codebook):
    block = block.astype(jnp.float32)
    cross_product = jnp.dot(codebook, block, precision=lax.Precision.HIGHEST)
    squared_norms = jnp.sum(codebook * codebook, axis=1)
    affinity_scores = (2.0 * cross_product - squared_norms[:, None]) / softness_scale
    weights = jax.nn.softmax(affinity_scores, axis=0)
    recon = jnp.dot(codebook.T, weights, precision=lax.Precision.HIGHEST)
    sums = lax.dot_general(
        weights, block, (((1,), (1,)), ((), ())), precision=lax.Precision.HIGHEST
    )
    counts = jnp.sum(weights, axis=1)
    return (recon, sums, counts)


def on_device(vectors, rotation, codebooks):
    row_count = vectors.shape[0]
    width = vectors.shape[1]
    groups = lax.axis_size("sub")
    group_width = width // groups
    rotated_t = lax.dot_general(
        rotation, vectors, (((0,), (1,)), ((), ())), preferred_element_type=jnp.float32
    ).astype(jnp.bfloat16)
    grouped = rotated_t.reshape(groups, group_width, row_count)
    received = lax.all_to_all(grouped, "sub", split_axis=0, concat_axis=2, tiled=True)
    columns = received.shape[2]
    blocks = received.reshape(group_width // SUBDIM, SUBDIM, columns)
    recon, sums_local, counts_local = lax.map(
        lambda pair: quantize_rows(pair[0], pair[1]), (blocks, codebooks)
    )
    recon_sent = recon.astype(jnp.bfloat16).reshape(1, group_width, columns)
    returned = lax.all_to_all(recon_sent, "sub", split_axis=2, concat_axis=0, tiled=True)
    recon_t = returned.reshape(width, row_count)
    total = row_count * lax.axis_size("row") * groups * lax.axis_size("rep")
    code_sums, counts = lax.psum((sums_local, counts_local), ("row", "rep"))
    partial_term = lax.dot_general(
        vectors, recon_t, (((0,), (1,)), ((), ())), preferred_element_type=jnp.float32
    )
    whole_cross = lax.psum(partial_term, ("row", "sub", "rep"))
    cross_rows = lax.dynamic_slice_in_dim(
        whole_cross, lax.axis_index("sub") * group_width, group_width, 0
    )
    new_codebooks = (code_sums + codebooks) / (counts[:, :, None] + 1.0)
    reconstruction = recon_t.T
    return (reconstruction, new_codebooks, cross_rows / total)


def solution(mesh):
    placed = (P(("dom", "row", "sub", "rep"), None), P("dom", None), P(("dom", "sub"), None, None))
    return jax.shard_map(
        on_device,
        mesh=mesh,
        in_specs=placed,
        out_specs=(
            P(("dom", "row", "sub", "rep"), None),
            P(("dom", "sub"), None, None),
            P(("dom", "sub"), None),
        ),
        check_vma=False,
    )
```

profile of v0, /device:TPU:0, one launch (start us, length us, event | category | flops | bytes accessed | tf_op | source)
XLA Modules:
  0.0 368.6 jit_solution(16869227199885064852)
XLA Ops:
  8.5 3.8 %convolution_convert_fusion = bf16[768,896]{1,0:T(8,128)(2,1)} fusion(bf16[768,768]{1,0:T(8,128)(2,1)} %param.6, bf16[896,768]{1,0:T(8,128)(2,1)S(1)} %copy-done), kind=kOutput, calls=%fused_computation.25 | convolution fusion | flops 1057652736 | bytes 3932160 | tf_op jit(solution)/shard_map/dot_general | solution.py:29
  12.3 4.2 %all-to-all-start = ((bf16[2,384,896]{2,1,0:T(8,128)(2,1)}), bf16[2,384,896]{2,1,0:T(8,128)(2,1)S(1)}, u32[]{:S(2)}, u32[]{:S(2)}) async-start(bf16[2,384,896]{2,1,0:T(8,128)(2,1)} %bitcast.68), calls=%async_computation | async-start | bytes 2752512 | tf_op jit(solution)/shard_map/all_to_all | solution.py:33
  16.5 18.0 %all-to-all-done = bf16[2,384,896]{2,1,0:T(8,128)(2,1)S(1)} async-done(((bf16[2,384,896]{2,1,0:T(8,128)(2,1)}), bf16[2,384,896]{2,1,0:T(8,128)(2,1)S(1)}, u32[]{:S(2)}, u32[]{:S(2)}) %all-to-all-start) | async-done | bytes 1376288 | tf_op jit(solution)/shard_map/all_to_all | solution.py:33
  34.5 2.5 copy.16
  37.0 3.5 reshape.26
  40.5 130.4 %while.14 = (s32[]{:T(128)}, bf16[24,16,1792]{2,1,0:T(8,128)(2,1)}, f32[24,256,16]{1,2,0:T(8,128)}, f32[24,256]{1,0:T(8,128)S(1)}, f32[24,256,16]{1,2,0:T(8,128)...) while((s32[]{:T(128)}, bf16[24,16,1792]{2,1,0:T(8,128)(2,1)}, f32[24,256,16]{1,2,0:T(8,128)}, ...), condition=%wide.region_5.6_spmd, body=%wide.region_0.5_spmd.sunk | while | flops 270209024 | bytes 9546853 | solution.py:36
  41.9 1.8 fusion.43
  47.4 1.8 fusion.43
  49.2 1.8 fusion.44
  52.8 1.8 fusion.43
  58.2 1.8 fusion.43
  63.7 1.8 fusion.43
  69.1 1.8 fusion.43
  70.9 1.8 fusion.44
  74.5 1.8 fusion.43
  80.0 1.8 fusion.43
  81.8 1.8 fusion.44
  85.4 1.8 fusion.43
  90.8 1.8 fusion.43
  96.3 1.8 fusion.43
  101.7 1.8 fusion.43
  103.5 1.8 fusion.44
  107.1 1.8 fusion.43
  112.6 1.8 fusion.43
  118.0 1.8 fusion.43
  123.4 1.8 fusion.43
  125.2 1.8 fusion.44
  128.9 1.8 fusion.43
  134.3 1.8 fusion.43
  136.1 1.8 fusion.44
  139.7 1.8 fusion.43
  145.2 1.8 fusion.43
  147.0 1.8 fusion.44
  150.6 1.8 fusion.43
  156.0 1.8 fusion.43
  161.5 1.8 fusion.43
  166.9 1.8 fusion.43
  170.9 7.0 %copy.17 = bf16[1,384,1792]{1,0,2:T(2,128)(2,1)} copy(bf16[1,384,1792]{2,1,0:T(8,128)(2,1)} %bitcast.67) | data formatting | bytes 2752512 | tf_op jit(solution)/shard_map/reshape | solution.py:39
  178.4 12.4 %reduce = bf16[1792,384]{1,0:T(8,128)(2,1)S(1)} reduce(bf16[1792,1,384]{2,1,0:T(2,128)(2,1)} %bitcast.61, bf16[]{:T(256)} %broadcast.16), dimensions={1}, to_apply=%bitcast.35.reduce_sub_computation | reduce | bytes 2752514
  192.0 3.6 all-to-all-start.1
  196.7 15.8 %all-to-all-done.1 = bf16[2,2,172032]{2,1,0:T(2,128)(2,1)S(1)} async-done(((bf16[2,2,172032]{2,1,0:T(2,128)(2,1)}), bf16[2,2,172032]{2,1,0:T(2,128)(2,1)S(1)}, u32[]{:S(2)}, u32[]{:S(2)}) %all-to-all-start.1) | async-done | bytes 1376288 | tf_op jit(solution)/shard_map/all_to_all | solution.py:40
  212.5 2.3 reshape.30
  214.8 3.1 copy.21
  219.7 2.8 convolution_bitcast_fusion.2
  222.5 27.0 %psum.22 = f32[24,256]{1,0:T(8,128)S(1)} all-reduce(f32[24,256]{1,0:T(8,128)S(1)} %get-tuple-element.39), channel_id=1, replica_groups=mesh['dom'=2,'row'=4,'sub'=2,'rep'=2] {'row','rep'}, use_global_device_ids=true, to_apply=%region_7.8 | all-reduce | flops 6144 | bytes 49152 | tf_op jit(solution)/shard_map/psum | solution.py:43
  249.5 7.6 %all-reduce.3.cloned.1.call-done = f32[24,256,16]{1,2,0:T(8,128)} async-done(((f32[24,256,16]{1,2,0:T(8,128)}), f32[24,256,16]{1,2,0:T(8,128)}) %all-reduce.3.cloned.1.call-update) | async-done | bytes 393232 | tf_op jit(solution)/shard_map/psum | solution.py:43
  257.1 1.8 add_divide_fusion
  260.4 98.6 %all-reduce.5.cloned.1.call-done = f32[768,768]{0,1:T(8,128)} async-done(((f32[768,768]{0,1:T(8,128)}), f32[768,768]{0,1:T(8,128)}) %all-reduce.5.cloned.1.call-update) | async-done | bytes 2359312 | tf_op jit(solution)/shard_map/psum | solution.py:47
  (155 shorter events, 83.7 us)
Async XLA Ops:
  7.2 1.3 copy-start
  12.3 22.2 %all-to-all-start = ((bf16[2,384,896]{2,1,0:T(8,128)(2,1)}), bf16[2,384,896]{2,1,0:T(8,128)(2,1)S(1)}, u32[]{:S(2)}, u32[]{:S(2)}) async-start(bf16[2,384,896]{2,1,0:T(8,128)(2,1)} %bitcast.68), calls=%async_computation | async-start | bytes 2752512 | tf_op jit(solution)/shard_map/all_to_all | solution.py:33
  37.0 3.5 copy-start.1
  192.0 20.5 %all-to-all-start.1 = ((bf16[2,2,172032]{2,1,0:T(2,128)(2,1)}), bf16[2,2,172032]{2,1,0:T(2,128)(2,1)S(1)}, u32[]{:S(2)}, u32[]{:S(2)}) async-start(bf16[2,2,172032]{2,1,0:T(2,128)(2,1)} %reshape.29), calls=%async_computation.1 | async-start | bytes 2752512 | tf_op jit(solution)/shard_map/all_to_all | solution.py:40
  195.7 61.4 %all-reduce.3.cloned.1.call-start = ((), (), s32[]{:S(2)}) async-start(), calls=%async_computation.2 | async-start | bytes 786432 | tf_op jit(solution)/shard_map/psum | solution.py:43
  196.4 162.6 %all-reduce.5.cloned.1.call-start = ((), (), s32[]{:S(2)}) async-start(), calls=%async_computation.3 | async-start | bytes 4718592 | tf_op jit(solution)/shard_map/psum | solution.py:47
Sparse Core Ops, SparseCore 0:
  199.4 57.6 all-reduce.2
  261.1 97.9 all-reduce.4
where the time goes:
time: 369 us
  waiting for transfers between devices  141 us (38%)
  matrix products  119 us (32%)
  other arithmetic  31.9 us (9%)
  local copies, waits for them, and re-layouts  27.1 us (7%)
  blocking collectives  27 us (7%)
  between operations  14.1 us (4%)
  starting transfers between devices  8.1 us (2%)
    psum x1, waiting for transfers between devices, on_device(): whole_cross = lax.psum(partial_term, ('row', 'sub', 'rep'))  98.6 us
    dot_general x24, matrix products, quantize_rows(): recon = jnp.dot(codebook.T, weights, precision=lax.Precision.HIGHEST)  43.4 us
    dot_general x24, matrix products, quantize_rows(): lax.dot_general(weights, block, (((1,), (1,)), ((), ())), precision=lax.P...  43.1 us
    psum x1, blocking collectives, on_device(): code_sums, counts = lax.psum((sums_local, counts_local), ('row', 'rep'))  27 us
    dot_general x24, matrix products, quantize_rows(): cross_product = jnp.dot(codebook, block, precision=lax.Precision.HIGHEST)  25.8 us
    all_to_all x1, waiting for transfers between devices, on_device(): lax.all_to_all(grouped, 'sub', split_axis=0, concat_axis=2, tiled=True)  18 us
    all_to_all x1, waiting for transfers between devices, on_device(): lax.all_to_all(recon_sent, 'sub', split_axis=2, concat_axis=0, tiled=True)  15.8 us
    unnamed x1, other arithmetic  12.4 us
  transfers between devices with their start and end apart: 4, of which 4 were waited for; matrix products, arithmetic and copies ran while one was open for 4% of the time, Pallas kernels for 0%

commit v1 on v0

--- a/solution.py
+++ b/solution.py
@@ -44,7 +44,7 @@
     partial_term = lax.dot_general(
         vectors, recon_t, (((0,), (1,)), ((), ())), preferred_element_type=jnp.float32
     )
-    whole_cross = lax.psum(partial_term, ("row", "sub", "rep"))
+    whole_cross = jnp.sum(lax.all_gather(partial_term, ("row", "sub", "rep")), axis=0)
     cross_rows = lax.dynamic_slice_in_dim(
         whole_cross, lax.axis_index("sub") * group_width, group_width, 0
     )

time: 369 us -> 467 us (1.27)
  waiting for transfers between devices: 141 us -> 197 us
  local copies, waits for them, and re-layouts: 27.1 us -> 49.1 us
  other arithmetic: 31.9 us -> 48.2 us
    psum x1, waiting for transfers between devices: 7.6 us -> 163 us  [on_device(): code_sums, counts = lax.psum((sums_local, counts_local), ('row', 'rep'))]
    psum x1 -> x0, waiting for transfers between devices: 98.6 us -> none  [on_device(): whole_cross = lax.psum(partial_term, ('row', 'sub', 'rep'))]
    unnamed x10 -> x13, local copies, waits for them, and re-layouts: 11.4 us -> 33.5 us
    reduce_sum x0 -> x1, other arithmetic: none -> 16.2 us  [on_device(): jnp.sum(lax.all_gather(partial_term, ('row', 'sub', 'rep')), axis=0)]
  transfers between devices with their start and end apart: 4 -> 4, of which waited for: 4 -> 3; matrix products, arithmetic and copies ran while one was open for 4% -> 3% of each run, Pallas kernels for 0% -> 0%
where the time goes in v1:
time: 467 us; the launch traced here: 466 us
  waiting for transfers between devices  197 us (42%)
  matrix products  119 us (25%)
  local copies, waits for them, and re-layouts  49.1 us (11%)
  other arithmetic  48.2 us (10%)
  blocking collectives  27.6 us (6%)
  between operations  15.6 us (3%)
  starting transfers between devices  8.11 us (2%)
    psum x1, waiting for transfers between devices, on_device(): code_sums, counts = lax.psum((sums_local, counts_local), ('row', 'rep'))  163 us
    dot_general x24, matrix products, quantize_rows(): recon = jnp.dot(codebook.T, weights, precision=lax.Precision.HIGHEST)  43.4 us
    dot_general x24, matrix products, quantize_rows(): lax.dot_general(weights, block, (((1,), (1,)), ((), ())), precision=lax.P...  43.1 us
    unnamed x13, local copies, waits for them, and re-layouts  33.5 us
    psum x1, blocking collectives, on_device(): code_sums, counts = lax.psum((sums_local, counts_local), ('row', 'rep'))  27.6 us
    dot_general x24, matrix products, quantize_rows(): cross_product = jnp.dot(codebook, block, precision=lax.Precision.HIGHEST)  25.8 us
    all_to_all x1, waiting for transfers between devices, on_device(): lax.all_to_all(grouped, 'sub', split_axis=0, concat_axis=2, tiled=True)  18 us
    reduce_sum x1, other arithmetic, on_device(): jnp.sum(lax.all_gather(partial_term, ('row', 'sub', 'rep')), axis=0)  16.2 us
  transfers between devices with their start and end apart: 4, of which 3 were waited for; matrix products, arithmetic and copies ran while one was open for 3% of the time, Pallas kernels for 0%

profile of v1, /device:TPU:0, one launch (start us, length us, event | category | flops | bytes accessed | tf_op | source)
XLA Modules:
  0.0 465.8 jit_solution(15914697148765320441)
XLA Ops:
  9.3 3.8 convolution_convert_fusion
  13.1 4.2 all-to-all-start
  17.3 18.0 %all-to-all-done = bf16[2,384,896]{2,1,0:T(8,128)(2,1)S(1)} async-done(((bf16[2,384,896]{2,1,0:T(8,128)(2,1)}), bf16[2,384,896]{2,1,0:T(8,128)(2,1)S(1)}, u32[]{:S(2)}, u32[]{:S(2)}) %all-to-all-start) | async-done | bytes 1376288 | tf_op jit(solution)/shard_map/all_to_all | solution.py:33
  35.3 2.5 copy.13
  37.8 3.5 reshape.26
  41.4 130.4 %while.14 = (s32[]{:T(128)}, bf16[24,16,1792]{2,1,0:T(8,128)(2,1)}, f32[24,256,16]{1,2,0:T(8,128)}, f32[24,256]{1,0:T(8,128)S(1)}, f32[24,256,16]{1,2,0:T(8,128)...) while((s32[]{:T(128)}, bf16[24,16,1792]{2,1,0:T(8,128)(2,1)}, f32[24,256,16]{1,2,0:T(8,128)}, ...), condition=%wide.region_5.6_spmd, body=%wide.region_0.5_spmd.sunk | while | flops 270209024 | bytes 9546853 | solution.py:36
  42.8 1.8 fusion.43
  48.2 1.8 fusion.43
  50.0 1.8 fusion.44
  53.6 1.8 fusion.43
  59.1 1.8 fusion.43
  60.9 1.8 fusion.44
  64.5 1.8 fusion.43
  69.9 1.8 fusion.43
  71.7 1.8 fusion.44
  75.4 1.8 fusion.43
  80.8 1.8 fusion.43
  86.2 1.8 fusion.43
  91.7 1.8 fusion.43
  93.5 1.8 fusion.44
  97.1 1.8 fusion.43
  102.5 1.8 fusion.43
  104.3 1.8 fusion.44
  108.0 1.8 fusion.43
  113.4 1.8 fusion.43
  118.8 1.8 fusion.43
  124.3 1.8 fusion.43
  126.1 1.8 fusion.44
  129.7 1.8 fusion.43
  135.1 1.8 fusion.43
  140.6 1.8 fusion.43
  146.0 1.8 fusion.43
  151.4 1.8 fusion.43
  156.8 1.8 fusion.43
  162.3 1.8 fusion.43
  167.7 1.8 fusion.43
  171.8 7.0 %copy.14 = bf16[1,384,1792]{1,0,2:T(2,128)(2,1)} copy(bf16[1,384,1792]{2,1,0:T(8,128)(2,1)} %bitcast.73) | data formatting | bytes 2752512 | tf_op jit(solution)/shard_map/reshape | solution.py:39
  179.2 12.4 %reduce = bf16[1792,384]{1,0:T(8,128)(2,1)S(1)} reduce(bf16[1792,1,384]{2,1,0:T(2,128)(2,1)} %bitcast.67, bf16[]{:T(256)} %broadcast.16), dimensions={1}, to_apply=%bitcast.40.reduce_sub_computation | reduce | bytes 2752514
  192.9 3.6 all-to-all-start.1
  197.5 15.8 %all-to-all-done.1 = bf16[2,2,172032]{2,1,0:T(2,128)(2,1)S(1)} async-done(((bf16[2,2,172032]{2,1,0:T(2,128)(2,1)}), bf16[2,2,172032]{2,1,0:T(2,128)(2,1)S(1)}, u32[]{:S(2)}, u32[]{:S(2)}) %all-to-all-start.1) | async-done | bytes 1376288 | tf_op jit(solution)/shard_map/all_to_all | solution.py:40
  213.3 2.3 reshape.31
  215.6 3.1 copy.18
  220.5 2.8 convolution_bitcast_fusion.2
  223.3 27.6 %psum.15 = f32[24,256]{1,0:T(8,128)S(1)} all-reduce(f32[24,256]{1,0:T(8,128)S(1)} %get-tuple-element.39), channel_id=1, replica_groups=mesh['dom'=2,'row'=4,'sub'=2,'rep'=2] {'row','rep'}, use_global_device_ids=true, to_apply=%region_7.8 | all-reduce | flops 6144 | bytes 49152 | tf_op jit(solution)/shard_map/psum | solution.py:43
  250.9 162.9 %all-reduce.2.cloned.1.call-done = f32[24,256,16]{1,2,0:T(8,128)} async-done(((f32[24,256,16]{1,2,0:T(8,128)}), f32[24,256,16]{1,2,0:T(8,128)}) %all-reduce.2.cloned.1.call-update) | async-done | bytes 393232 | tf_op jit(solution)/shard_map/psum | solution.py:43
  413.9 1.9 add_divide_fusion
  417.3 22.0 %copy.19 = f32[96,8,16,768]{3,2,1,0:T(8,128)S(1)} copy(f32[96,8,16,768]{3,1,2,0:T(8,128)} %bitcast.66) | data formatting | bytes 75497472
  439.4 16.2 %bitcast_reduce_fusion = f32[768,768]{0,1:T(8,128)} fusion(f32[96,8,16,768]{3,2,1,0:T(8,128)S(1)} %copy.19), kind=kLoop, calls=%fused_computation.24 | loop fusion | flops 8847360 | bytes 40108032 | tf_op jit(solution)/shard_map/reduce_sum | solution.py:47
  (159 shorter events, 85.6 us)
Async XLA Ops:
  8.0 1.3 copy-start
  13.1 22.2 %all-to-all-start = ((bf16[2,384,896]{2,1,0:T(8,128)(2,1)}), bf16[2,384,896]{2,1,0:T(8,128)(2,1)S(1)}, u32[]{:S(2)}, u32[]{:S(2)}) async-start(bf16[2,384,896]{2,1,0:T(8,128)(2,1)} %bitcast.74), calls=%async_computation | async-start | bytes 2752512 | tf_op jit(solution)/shard_map/all_to_all | solution.py:33
  37.8 3.5 copy-start.2
  192.9 20.4 %all-to-all-start.1 = ((bf16[2,2,172032]{2,1,0:T(2,128)(2,1)}), bf16[2,2,172032]{2,1,0:T(2,128)(2,1)S(1)}, u32[]{:S(2)}, u32[]{:S(2)}) async-start(bf16[2,2,172032]{2,1,0:T(2,128)(2,1)} %reshape.30), calls=%async_computation.1 | async-start | bytes 2752512 | tf_op jit(solution)/shard_map/all_to_all | solution.py:40
  196.5 217.4 %all-reduce.2.cloned.1.call-start = ((), (), s32[]{:S(2)}) async-start(), calls=%async_computation.2 | async-start | bytes 786432 | tf_op jit(solution)/shard_map/psum | solution.py:43
  197.3 220.1 %all-gather.3.cloned.1.call-start = ((), (), s32[]{:S(2)}) async-start(), calls=%async_computation.3 | async-start | bytes 40108032 | tf_op jit(solution)/shard_map/all_gather | solution.py:47
  439.4 19.0 %copy-start.1 = (bf16[896,768]{1,0:T(8,128)(2,1)S(1)}, bf16[896,768]{1,0:T(8,128)(2,1)}, u32[]{:S(2)}) copy-start(bf16[896,768]{1,0:T(8,128)(2,1)} %param.5) | copy-start | bytes 4128772
Sparse Core Ops, SparseCore 0:
  200.3 213.5 all-reduce.1
Sparse Core Ops, SparseCore 1:
  223.4 192.1 all-gather.2
